TPU v7x, 32 devices: a whole 2x2x4 slice. The times are simulated.
32 devices in a mesh: groups: 2 (over x), utt: 16 (over z, y, core).
Axes of the slice: x: 2, y: 2, z: 4, core: 2. Of those that a mesh axis runs over, the one named last changes fastest.
Arguments:
- waveforms: float32 [64, 90], P(('groups', 'utt')), parts along dimension 0, may hold values from -6 to 6
- lengths: int32 [64], P(('groups', 'utt')), parts along dimension 0, may hold values from 1 to 7, as said below
- take_list: int32 [64], P(('groups', 'utt')), parts along dimension 0, may hold values from 0 to 31, as said below
- conv_first: float32 [3, 10, 512], replicated, may hold values from -2 to 2
- conv_second: bfloat16 [3, 1536, 512], replicated, may hold values from -0.15625 to 0.15625
- norm_gain: float32 [3, 2, 512], replicated, may hold values from 0.5 to 1.5
- norm_shift: float32 [3, 2, 512], replicated, may hold values from -2 to 2
- enc_weight: bfloat16 [1536, 8192], P(None, 'utt'), may hold values from -0.15625 to 0.15625
- enc_bias: float32 [8192], P('utt'), may hold values from -2 to 2
- dec_weight: bfloat16 [8192, 1536], P('utt'), may hold values from -0.0625 to 0.0625
- dec_bias: float32 [1536], replicated, may hold values from -2 to 2
Outputs:
- enc_grad: bfloat16 [3072, 8192], P('groups', 'utt'), parts along dimension 0
- dec_grad: bfloat16 [16384, 1536], P(('groups', 'utt')), parts along dimension 0
- enc_bias_grad: float32 [16384], P(('groups', 'utt')), parts along dimension 0
- dec_bias_grad: float32 [3072], P('groups'), parts along dimension 0
- mean_loss: float32 [2], P('groups'), parts along dimension 0
- errors_out: bfloat16 [256, 1536], P(('groups', 'utt')), parts along dimension 0
There are 2 independent parts, one for each index of `groups`. A program takes and returns all parts, laid end to end along the dimension named above; an argument that names none is the same for every part. Nothing has to cross between parts.
Inputs may be any that keep to these rules, and one draw needn't show every extreme that they name: Valid frames of each utterance; the 32 lengths sum to 128, and some utterance has exactly 7. `take_list`: a permutation of the utterances: entry d * 2 + k names the utterance that slot k of device d takes; the utterances taken by the slots of one device have 8 valid frames together.
All inputs are finite; a program needn't handle non-finite values.
Results may differ from a plain program's by a relative error of at most 0.0095.
Values may be sent and summed in bfloat16 or wider, within the bound.
No kernel may reach another device: no remote copies, remote signals or barrier semaphores. Data moves between devices by JAX's collectives and lax.ppermute only.
A program may use at most 128 MiB of HBM per device.

v0:
```python
import jax
import jax.numpy as jnp
from jax import lax
from jax.sharding import PartitionSpec as P

ROWS_DEV = 8
sparsity = 0.5
epsilon = 1e-05


def normalize(values, gain, shift):
    center = values - jnp.mean(values, axis=-1, keepdims=True)
    spread = jnp.mean(center * center, axis=-1, keepdims=True)
    return center * lax.rsqrt(spread + epsilon) * gain + shift


def extract(chosen, conv_first, conv_second, norm_gain, norm_shift):
    count = chosen.shape[0]
    frames = (chosen.shape[1] - 10) // 10
    checkpoints = conv_first.shape[0]
    channels = conv_first.shape[2]
    blocks = chosen.reshape(count, 2 * frames + 2, 5)
    windows = jnp.concatenate([blocks[:, :-1], blocks[:, 1:]], axis=-1)
    first = jnp.einsum("ntk,ckd->cntd", windows, conv_first, precision=lax.Precision.HIGHEST)
    first = normalize(first, norm_gain[:, 0][:, None, None, :], norm_shift[:, 0][:, None, None, :])
    first = jax.nn.gelu(first, approximate=False).astype(jnp.bfloat16)
    paired = first[:, :, :-1].reshape(checkpoints, count, frames, 2 * channels)
    columns = jnp.concatenate([paired, first[:, :, 2::2]], axis=-1)
    second = jnp.einsum("cntk,ckd->cntd", columns, conv_second, preferred_element_type=jnp.float32)
    second = normalize(
        second, norm_gain[:, 1][:, None, None, :], norm_shift[:, 1][:, None, None, :]
    )
    second = jax.nn.gelu(second, approximate=False).astype(jnp.bfloat16)
    return second.transpose(1, 2, 0, 3).reshape(count, frames, checkpoints * channels)


def shards(
    waveforms,
    lengths,
    take_list,
    conv_first,
    conv_second,
    norm_gain,
    norm_shift,
    enc_weight,
    enc_bias,
    dec_weight,
    dec_bias,
):
    slots = take_list.shape[0]
    devices = lax.axis_size("utt")
    tokens = ROWS_DEV * devices
    position = lax.axis_index("utt")
    piece_sound = lax.all_gather(waveforms, "utt", axis=0, tiled=True)
    piece_length = lax.all_gather(lengths, "utt", axis=0, tiled=True)
    labels = jnp.arange(piece_sound.shape[0], dtype=jnp.int32)
    match = take_list[:, None] == labels[None, :]
    sound_sum = jnp.dot(match.astype(jnp.float32), piece_sound, precision=lax.Precision.HIGHEST)
    length_sum = jnp.sum(jnp.where(match, piece_length[None, :], 0), axis=1).astype(jnp.int32)
    frames = extract(sound_sum, conv_first, conv_second, norm_gain, norm_shift)
    frame_count = frames.shape[1]
    feature = frames.shape[2]
    flat_frames = frames.reshape(slots * frame_count, feature)
    local_start = jnp.cumsum(length_sum) - length_sum
    frame_index = jnp.arange(frame_count, dtype=jnp.int32)
    valid = frame_index[None, :] < length_sum[:, None]
    before = position * ROWS_DEV
    targets = jnp.where(valid, before + local_start[:, None] + frame_index[None, :], tokens)
    targets = targets.reshape(-1)
    all_frames, all_targets = (
        lax.all_gather(flat_frames, "utt", axis=0, tiled=True),
        lax.all_gather(targets, "utt", axis=0, tiled=True),
    )
    inputs = jnp.zeros((tokens + 1, feature), jnp.bfloat16).at[all_targets].set(all_frames)[:tokens]
    latents_dev = enc_weight.shape[1]
    checkpoints = conv_first.shape[0]
    channels = conv_first.shape[2]
    preact = jnp.dot(inputs, enc_weight, preferred_element_type=jnp.float32) + enc_bias
    latent = jnp.maximum(preact, 0.0)
    latent_b = latent.astype(jnp.bfloat16)
    decoder = dec_weight.astype(jnp.float32).reshape(latents_dev, checkpoints, channels)
    norms = jnp.sqrt(jnp.sum(decoder * decoder, axis=-1) + 1e-06)
    weights_sum = jnp.sum(norms, axis=-1)
    partial_recon = jnp.dot(latent_b, dec_weight, preferred_element_type=jnp.float32)
    recon = lax.psum(partial_recon, "utt")
    errors = recon + dec_bias - inputs.astype(jnp.float32)
    errors_b = errors.astype(jnp.bfloat16)
    own_errors = lax.dynamic_slice_in_dim(errors, position * ROWS_DEV, ROWS_DEV, 0)
    loss_part = jnp.sum(own_errors * own_errors) + sparsity * jnp.sum(latent * weights_sum)
    bias_part = jnp.sum(2.0 * own_errors, axis=0)
    dec_bias_grad, loss_total = lax.psum((bias_part, loss_part), "utt")
    mean_loss = (loss_total / (tokens * feature)).reshape(1)
    activity = jnp.sum(latent, axis=0)
    dec_grad = 2.0 * jnp.dot(latent_b.T, errors_b, preferred_element_type=jnp.float32)
    dec_grad = dec_grad + sparsity * (
        activity[:, None, None] * decoder / norms[:, :, None]
    ).reshape(latents_dev, feature)
    upstream = (
        2.0 * jnp.dot(errors_b, dec_weight.T, preferred_element_type=jnp.float32)
        + sparsity * weights_sum
    )
    through = jnp.where(preact > 0.0, upstream, 0.0)
    enc_grad = jnp.dot(inputs.T, through.astype(jnp.bfloat16), preferred_element_type=jnp.float32)
    return (
        enc_grad.astype(jnp.bfloat16),
        dec_grad.astype(jnp.bfloat16),
        jnp.sum(through, axis=0),
        dec_bias_grad,
        mean_loss,
        own_errors.astype(jnp.bfloat16),
    )


def solution(mesh):
    return jax.shard_map(
        shards,
        mesh=mesh,
        in_specs=(
            P(("groups", "utt"), None),
            P(("groups", "utt")),
            P(("groups", "utt")),
            P(),
            P(),
            P(),
            P(),
            P(None, "utt"),
            P("utt"),
            P("utt", None),
            P(),
        ),
        out_specs=(
            P("groups", "utt"),
            P(("groups", "utt"), None),
            P(("groups", "utt")),
            P("groups"),
            P("groups"),
            P(("groups", "utt"), None),
        ),
        check_vma=False,
    )
```

profile of v0, /device:TPU:0, one launch (start us, length us, event | category | flops | bytes accessed | tf_op | source)
XLA Modules:
  0.0 240.3 jit_solution(2240350737570929996)
XLA Ops:
  7.2 0.0 copy-start
  7.2 0.0 all-reduce.5.cloned.1.call-start
  7.2 23.5 %all-gather = f32[16,2,90]{2,1,0:T(2,128)S(1)} all-gather(f32[1,2,90]{2,1,0:T(2,128)} %bitcast.74), channel_id=1, replica_groups=mesh['groups'=2,'utt'=16] {'utt'}, dimensions={0}, use_global_device_ids=true | all-gather | bytes 12240 | tf_op jit(solution)/shard_map/all_gather | solution.py:54
  30.7 0.8 fusion.44
  31.6 0.1 reshape.106
  31.7 0.1 copy.53
  31.8 0.1 copy.54
  31.8 1.4 fusion.55
  33.3 0.2 multiply_reduce_fusion
  33.5 0.8 fusion.54
  34.3 0.8 fusion.53
  35.1 0.8 fusion.12
  35.9 0.1 slice.32
  36.1 0.0 copy-start.8
  36.1 0.0 copy-start.6
  36.1 0.0 copy-start.7
  36.1 0.0 copy-start.1
  36.1 3.3 %fusion.56 = (f32[3,2,8]{2,1,0:T(2,128)S(1)}, f32[3,2,8,512]{3,2,1,0:T(8,128)S(1)}) fusion(bf16[3,1536,512]{2,1,0:T(8,128)(2,1)} %param.15, bf16[3,2,8,512]{3,2,0,1:T(8,128)(2,1)S(1)} %slice.32, bf16[3,2,8,1024]{3,2,0,1:T(8,128)(2,1)S(1)} %reshape.107), kind=kOutput, calls=%fused_computation.111 | convolution fusion | flops 75816912 | bytes 4964544 | tf_op jit(solution)/shard_map/cntk,ckd->cntd/dot_general | solution.py:29
  39.4 0.2 multiply_reduce_fusion.2
  39.6 0.3 fusion.28
  40.0 21.0 %all_gather.15 = bf16[256,1536]{1,0:T(8,128)(2,1)} all-gather(bf16[16,1536]{1,0:T(8,128)(2,1)S(1)} %bitcast.71), channel_id=1, replica_groups=mesh['groups'=2,'utt'=16] {'utt'}, dimensions={0}, use_global_device_ids=true | all-gather | bytes 835584 | tf_op jit(solution)/shard_map/all_gather | solution.py:71
  61.0 0.0 copy-done.8
  61.0 0.6 dynamic-slice
  62.2 0.0 copy-done.6
  62.2 0.2 dynamic-update-slice
  62.5 9.6 %all-reduce = s32[32]{0:T(128)S(1)} all-reduce(s32[32]{0:T(128)S(1)} %dynamic-update-slice), channel_id=1, replica_groups=mesh['groups'=2,'utt'=16] {'utt'}, use_global_device_ids=true, to_apply=%add | all-reduce | flops 32 | bytes 256
  72.1 0.0 copy-done.7
  72.1 0.2 select_reduce_fusion
  72.3 0.2 reduce-window.8
  72.5 0.1 compare_select_fusion.1
  72.5 0.1 reshape.121
  73.3 0.2 dynamic-update-slice.1
  73.5 11.2 %all-reduce.1 = s32[256]{0:T(256)S(1)} all-reduce(s32[256]{0:T(256)S(1)} %dynamic-update-slice.1), channel_id=1, replica_groups=mesh['groups'=2,'utt'=16] {'utt'}, use_global_device_ids=true, to_apply=%add.1 | all-reduce | flops 256 | bytes 2048
  84.8 0.0 copy-done.1
  84.8 2.1 convert_multiply_fusion.1
  86.9 3.6 %copy.44 = f32[512,1536]{0,1:T(8,128)} copy(f32[512,1536]{1,0:T(8,128)} %convert_multiply_fusion.1) | data formatting | bytes 6291456 | tf_op jit(solution)/shard_map/mul | solution.py:82
  90.5 0.0 copy-start.5
  90.5 2.1 reduce_sum.113
  92.6 3.1 %scatter_custom_fusion = bf16[129,1536]{1,0:T(8,128)(2,1)} fusion(s32[256]{0:T(256)S(1)} %compare_select_fusion, bf16[256,1536]{1,0:T(8,128)(2,1)} %all_gather.15, bf16[]{:T(256)} %constant.40.clone.1), kind=kCustom, calls=%fused_computation.43 | custom fusion | bytes 396800 | tf_op jit(solution)/shard_map/scatter | solution.py:74
  95.7 0.0 copy-done
  95.7 0.0 copy-done.5
  95.7 2.0 multiply_reduce_fusion.1
  97.7 1.3 fusion.41
  99.0 0.0 all-reduce.5.cloned.1.call-update
  99.0 2.1 div.33
  101.1 0.0 copy-start.4
  101.1 3.6 %copy.45 = f32[512,1536]{1,0:T(8,128)} copy(f32[512,1536]{0,1:T(8,128)} %bitcast.70) | data formatting | bytes 6291456 | tf_op jit(solution)/shard_map/div | solution.py:96
  105.4 83.7 %all-reduce.5.cloned.1.call-done = f32[128,1536]{1,0:T(8,128)} async-done(((f32[128,1536]{1,0:T(8,128)}), f32[128,1536]{1,0:T(8,128)}) %all-reduce.5.cloned.1.call-update) | async-done | bytes 786448 | tf_op jit(solution)/shard_map/psum | solution.py:85
  189.1 0.0 copy-done.4
  189.1 0.0 copy-start.2
  189.1 1.4 convert_subtract_fusion
  190.5 0.0 copy-start.3
  190.5 0.7 multiply_reduce_fusion.3
  191.3 0.6 dynamic-slice_convert_fusion
  191.9 1.3 fusion.57
  193.1 0.0 copy-done.2
  193.1 1.7 convolution_convert_fusion
  194.9 0.0 copy-done.3
  195.5 31.9 %all-reduce.2 = (f32[1536]{0:T(1024)}, f32[]{:T(128)}) all-reduce(f32[1536]{0:T(1024)S(1)} %get-tuple-element.7, f32[]{:T(128)S(6)} %add.150), channel_id=1, replica_groups=mesh['groups'=2,'utt'=16] {'utt'}, use_global_device_ids=true, to_apply=%region_13.14 | all-reduce | flops 1537 | bytes 12296 | tf_op jit(solution)/shard_map/psum | solution.py:91
  228.1 4.2 %fusion.5 = bf16[512,1536]{1,0:T(8,128)(2,1)} fusion(f32[512,1536]{1,0:T(8,128)} %copy.45, bf16[512,1536]{1,0:T(8,128)(2,1)S(1)} %copy-done.1, f32[512]{0:T(512)S(1)} %get-tuple-element.9, f32[128,1536]{1,0:T(8,128)} %copy-done.3, f32[128,512]{1,0:T(8,128)S(1)} %get-tuple-element.26), kind=kOutput, calls=%fused_computation.9 | convolution fusion | flops 207159296 | bytes 7342080 | tf_op jit(solution)/shard_map/dot_general | solution.py:94
  (17 shorter events, 0.2 us)
Async XLA Ops:
  7.2 88.5 %copy-start = (bf16[1536,512]{1,0:T(8,128)(2,1)S(1)}, bf16[1536,512]{1,0:T(8,128)(2,1)}, u32[]{:S(2)}) copy-start(bf16[1536,512]{1,0:T(8,128)(2,1)} %param.18) | copy-start | bytes 4718596
  7.2 181.9 %all-reduce.5.cloned.1.call-start = ((), (), s32[]{:S(2)}) async-start(), calls=%async_computation | async-start | bytes 1572864 | tf_op jit(solution)/shard_map/psum | solution.py:85
  36.1 24.9 %copy-start.8 = (u32[32]{0:T(128)S(1)}, u32[32]{0:T(128)}, u32[]{:S(2)}) copy-start(u32[32]{0:T(128)} %constant.13) | copy-start | bytes 388
  36.1 26.1 %copy-start.6 = (s32[2]{0:T(128)S(1)}, s32[2]{0:T(128)}, u32[]{:S(2)}) copy-start(s32[2]{0:T(128)} %param.12) | copy-start | bytes 28
  36.1 36.0 %copy-start.7 = (s32[2]{0:T(128)S(1)}, s32[2]{0:T(128)}, u32[]{:S(2)}) copy-start(s32[2]{0:T(128)} %param.13) | copy-start | bytes 28
  36.1 48.7 %copy-start.1 = (bf16[512,1536]{1,0:T(8,128)(2,1)S(1)}, bf16[512,1536]{1,0:T(8,128)(2,1)}, u32[]{:S(2)}) copy-start(bf16[512,1536]{1,0:T(8,128)(2,1)} %param.20) | copy-start | bytes 4718596
  90.5 5.3 %copy-start.5 = (f32[512]{0:T(512)S(1)}, f32[512]{0:T(512)}, u32[]{:S(2)}) copy-start(f32[512]{0:T(512)} %param.19) | copy-start | bytes 6148
  101.1 88.0 %copy-start.4 = (f32[1536]{0:T(1024)S(1)}, f32[1536]{0:T(1024)}, u32[]{:S(2)}) copy-start(f32[1536]{0:T(1024)} %param.21) | copy-start | bytes 18436
  189.1 4.0 %copy-start.2 = (bf16[129,1536]{1,0:T(8,128)(2,1)S(1)}, bf16[129,1536]{1,0:T(8,128)(2,1)}, u32[]{:S(2)}) copy-start(bf16[129,1536]{1,0:T(8,128)(2,1)} %scatter_custom_fusion) | copy-start | bytes 1188868
  190.5 4.4 %copy-start.3 = (f32[128,1536]{1,0:T(8,128)}, f32[128,1536]{1,0:T(8,128)S(1)}, u32[]{:S(2)}) copy-start(f32[128,1536]{1,0:T(8,128)S(1)} %convert_subtract_fusion) | copy-start | bytes 2359300
Sparse Core Ops, SparseCore 0:
  99.1 89.9 all-reduce.4
where the time goes:
time: 241 us; the launch traced here: 240 us
  blocking collectives  97.2 us (40%)
  waiting for transfers between devices  83.8 us (35%)
  between operations  18.7 us (8%)
  local copies, waits for them, and re-layouts  16.3 us (7%)
  matrix products  16 us (7%)
  other arithmetic  8.29 us (3%)
    psum x1, waiting for transfers between devices, shards(): recon = lax.psum(partial_recon, 'utt')  83.7 us
    psum x1, blocking collectives, shards(): dec_bias_grad, loss_total = lax.psum((bias_part, loss_part), 'utt')  31.9 us
    all_gather x1, blocking collectives, shards(): piece_sound = lax.all_gather(waveforms, 'utt', axis=0, tiled=True)  23.5 us
    all_gather x1, blocking collectives, shards(): lax.all_gather(flat_frames, 'utt', axis=0, tiled=True)  21 us
    unnamed x2, blocking collectives  20.8 us
    div x2, local copies, waits for them, and re-layouts, shards(): activity[:, None, None] * decoder / norms[:, :, None]  5.7 us
  transfers between devices with their start and end apart: 1, of which 1 were waited for; matrix products, arithmetic and copies ran while one was open for 2% of the time, Pallas kernels for 0%

commit v1 on v0

--- a/solution.py
+++ b/solution.py
@@ -1,3 +1,4 @@
+import functools
 import jax
 import jax.numpy as jnp
 from jax import lax
@@ -6,6 +7,14 @@
 ROWS_DEV = 8
 sparsity = 0.5
 epsilon = 1e-05
+
+
+def meshes_detail(x_local, ax_name):
+    e_next = jnp.sum(jax.lax.all_gather(x_local, axis_name=ax_name), 0)
+    return e_next
+
+
+detail_lines = functools.partial(meshes_detail, ax_name="utt")
 
 
 def normalize(values, gain, shift):
@@ -82,7 +91,7 @@
     norms = jnp.sqrt(jnp.sum(decoder * decoder, axis=-1) + 1e-06)
     weights_sum = jnp.sum(norms, axis=-1)
     partial_recon = jnp.dot(latent_b, dec_weight, preferred_element_type=jnp.float32)
-    recon = lax.psum(partial_recon, "utt")
+    recon = detail_lines(partial_recon)
     errors = recon + dec_bias - inputs.astype(jnp.float32)
     errors_b = errors.astype(jnp.bfloat16)
     own_errors = lax.dynamic_slice_in_dim(errors, position * ROWS_DEV, ROWS_DEV, 0)

time: 241 us -> 258 us (1.071)
  waiting for transfers between devices: 83.8 us -> 92.5 us
  other arithmetic: 8.29 us -> 15.7 us
    all_gather x0 -> x1, waiting for transfers between devices: none -> 92.5 us  [meshes_detail(): e_next = jnp.sum(jax.lax.all_gather(x_local, axis_name=ax_name), 0)]
    psum x1 -> x0, waiting for transfers between devices: 83.7 us -> none  [shards(): recon = lax.psum(partial_recon, 'utt')]
    reduce_sum x0 -> x1, other arithmetic: none -> 6.76 us  [meshes_detail(): e_next = jnp.sum(jax.lax.all_gather(x_local, axis_name=ax_name), 0)]
where the time goes in v1:
time: 258 us
  blocking collectives  97.4 us (38%)
  waiting for transfers between devices  92.5 us (36%)
  between operations  18.6 us (7%)
  local copies, waits for them, and re-layouts  17.5 us (7%)
  matrix products  16 us (6%)
  other arithmetic  15.7 us (6%)
    all_gather x1, waiting for transfers between devices, meshes_detail(): e_next = jnp.sum(jax.lax.all_gather(x_local, axis_name=ax_name), 0)  92.5 us
    psum x1, blocking collectives, shards(): dec_bias_grad, loss_total = lax.psum((bias_part, loss_part), 'utt')  32.3 us
    all_gather x1, blocking collectives, shards(): piece_sound = lax.all_gather(waveforms, 'utt', axis=0, tiled=True)  23.4 us
    all_gather x1, blocking collectives, shards(): lax.all_gather(flat_frames, 'utt', axis=0, tiled=True)  21.5 us
    unnamed x2, blocking collectives  20.2 us
    reduce_sum x1, other arithmetic, meshes_detail(): e_next = jnp.sum(jax.lax.all_gather(x_local, axis_name=ax_name), 0)  6.76 us
    div x2, local copies, waits for them, and re-layouts, shards(): activity[:, None, None] * decoder / norms[:, :, None]  5.61 us
  transfers between devices with their start and end apart: 1, of which 1 were waited for; matrix products, arithmetic and copies ran while one was open for 2% of the time, Pallas kernels for 0%

profile of v1, /device:TPU:0, one launch (start us, length us, event | category | flops | bytes accessed | tf_op | source)
XLA Modules:
  0.0 257.7 jit_solution(2869941331871506544)
XLA Ops:
  7.2 0.0 copy-start
  7.2 0.0 all-gather.4.cloned.1.call-start
  7.2 0.8 fusion.53
  8.1 0.8 fusion.54
  8.9 23.4 %all-gather.1 = f32[16,2,90]{2,1,0:T(2,128)S(1)} all-gather(f32[1,2,90]{2,1,0:T(2,128)} %bitcast.77), channel_id=1, replica_groups=mesh['groups'=2,'utt'=16] {'utt'}, dimensions={0}, use_global_device_ids=true | all-gather | bytes 12240 | tf_op jit(solution)/shard_map/all_gather | solution.py:63
  32.2 0.8 fusion.44
  33.1 0.1 reshape.106
  33.2 0.1 copy.53
  33.3 0.1 copy.54
  33.4 1.4 fusion.55
  34.8 0.2 multiply_reduce_fusion
  35.0 0.8 fusion.12
  35.8 0.1 slice.32
  36.0 1.2 dynamic-slice
  38.5 0.9 dynamic-update-slice
  39.4 7.1 %all-reduce = s32[32]{0:T(128)S(1)} all-reduce(s32[32]{0:T(128)S(1)} %dynamic-update-slice), channel_id=1, replica_groups=mesh['groups'=2,'utt'=16] {'utt'}, use_global_device_ids=true, to_apply=%add | all-reduce | flops 32 | bytes 256
  46.5 0.8 select_reduce_fusion
  47.3 0.2 reduce-window.8
  47.5 0.1 compare_select_fusion.1
  47.6 0.1 reshape.122
  47.7 0.2 dynamic-update-slice.1
  47.9 13.0 %all-reduce.1 = s32[256]{0:T(256)S(1)} all-reduce(s32[256]{0:T(256)S(1)} %dynamic-update-slice.1), channel_id=1, replica_groups=mesh['groups'=2,'utt'=16] {'utt'}, use_global_device_ids=true, to_apply=%add.1 | all-reduce | flops 256 | bytes 2048
  61.0 0.0 copy-start.1
  61.0 3.3 %fusion.56 = (f32[3,2,8]{2,1,0:T(2,128)S(1)}, f32[3,2,8,512]{3,2,1,0:T(8,128)S(1)}) fusion(bf16[3,1536,512]{2,1,0:T(8,128)(2,1)} %param.15, bf16[3,2,8,512]{3,2,0,1:T(8,128)(2,1)S(1)} %slice.32, bf16[3,2,8,1024]{3,2,0,1:T(8,128)(2,1)S(1)} %reshape.107), kind=kOutput, calls=%fused_computation.111 | convolution fusion | flops 75816912 | bytes 4964544 | tf_op jit(solution)/shard_map/cntk,ckd->cntd/dot_general | solution.py:38
  64.3 0.2 multiply_reduce_fusion.2
  64.4 0.3 fusion.28
  64.8 21.5 %all_gather.21 = bf16[256,1536]{1,0:T(8,128)(2,1)} all-gather(bf16[16,1536]{1,0:T(8,128)(2,1)S(1)} %bitcast.74), channel_id=1, replica_groups=mesh['groups'=2,'utt'=16] {'utt'}, dimensions={0}, use_global_device_ids=true | all-gather | bytes 835584 | tf_op jit(solution)/shard_map/all_gather | solution.py:80
  86.4 0.0 copy-done.1
  86.4 2.1 convert_multiply_fusion.1
  88.5 3.6 %copy.44 = f32[512,1536]{0,1:T(8,128)} copy(f32[512,1536]{1,0:T(8,128)} %convert_multiply_fusion.1) | data formatting | bytes 6291456 | tf_op jit(solution)/shard_map/mul | solution.py:91
  92.0 0.0 copy-start.5
  92.0 2.1 reduce_sum.123
  94.2 3.1 %scatter_custom_fusion = bf16[129,1536]{1,0:T(8,128)(2,1)} fusion(s32[256]{0:T(256)S(1)} %compare_select_fusion, bf16[256,1536]{1,0:T(8,128)(2,1)} %all_gather.21, bf16[]{:T(256)} %constant.40.clone.1), kind=kCustom, calls=%fused_computation.43 | custom fusion | bytes 396800 | tf_op jit(solution)/shard_map/scatter | solution.py:83
  97.3 0.0 copy-done
  97.3 0.0 copy-done.5
  97.3 2.0 multiply_reduce_fusion.1
  99.3 1.3 fusion.41
  100.6 0.0 all-gather.4.cloned.1.call-update
  100.6 2.1 div.33
  102.7 3.6 %copy.45 = f32[512,1536]{1,0:T(8,128)} copy(f32[512,1536]{0,1:T(8,128)} %bitcast.72) | data formatting | bytes 6291456 | tf_op jit(solution)/shard_map/div | solution.py:105
  106.9 92.5 %all-gather.4.cloned.1.call-done = f32[2048,1536]{1,0:T(8,128)} async-done(((f32[128,1536]{1,0:T(8,128)}), f32[2048,1536]{1,0:T(8,128)}) %all-gather.4.cloned.1.call-update) | async-done | bytes 12582928 | tf_op jit(solution)/shard_map/all_gather | solution.py:13
  199.4 0.0 copy-start.4
  199.4 6.8 %reduce_sum.122 = f32[128,1536]{1,0:T(8,128)} reduce(f32[16,128,1536]{2,1,0:T(8,128)} %bitcast.73, f32[]{:T(128)} %constant.46.clone.1), dimensions={0}, to_apply=%region_7.8 | reduce | flops 2949120 | bytes 13369348 | tf_op jit(solution)/shard_map/reduce_sum | solution.py:13
  206.1 0.0 copy-done.4
  206.1 0.0 copy-start.2
  206.1 1.4 convert_subtract_fusion
  207.5 0.0 copy-start.3
  207.5 0.7 multiply_reduce_fusion.3
  208.3 0.6 dynamic-slice_convert_fusion
  208.9 1.3 fusion.57
  210.1 0.0 copy-done.2
  210.1 1.7 convolution_convert_fusion
  211.9 0.0 copy-done.3
  212.5 32.3 %all-reduce.2 = (f32[1536]{0:T(1024)}, f32[]{:T(128)}) all-reduce(f32[1536]{0:T(1024)S(1)} %get-tuple-element.7, f32[]{:T(128)S(6)} %add.148), channel_id=1, replica_groups=mesh['groups'=2,'utt'=16] {'utt'}, use_global_device_ids=true, to_apply=%region_13.14 | all-reduce | flops 1537 | bytes 12296 | tf_op jit(solution)/shard_map/psum | solution.py:100
  245.5 4.2 %fusion.5 = bf16[512,1536]{1,0:T(8,128)(2,1)} fusion(f32[512,1536]{1,0:T(8,128)} %copy.45, bf16[512,1536]{1,0:T(8,128)(2,1)S(1)} %copy-done.1, f32[512]{0:T(512)S(1)} %get-tuple-element.9, f32[128,1536]{1,0:T(8,128)} %copy-done.3, f32[128,512]{1,0:T(8,128)S(1)} %get-tuple-element.26), kind=kOutput, calls=%fused_computation.9 | convolution fusion | flops 207159296 | bytes 7342080 | tf_op jit(solution)/shard_map/dot_general | solution.py:103
  (17 shorter events, 0.2 us)
Async XLA Ops:
  7.2 90.1 %copy-start = (bf16[1536,512]{1,0:T(8,128)(2,1)S(1)}, bf16[1536,512]{1,0:T(8,128)(2,1)}, u32[]{:S(2)}) copy-start(bf16[1536,512]{1,0:T(8,128)(2,1)} %param.18) | copy-start | bytes 4718596
  7.2 192.2 %all-gather.4.cloned.1.call-start = ((), (), s32[]{:S(2)}) async-start(), calls=%async_computation | async-start | bytes 13369344 | tf_op jit(solution)/shard_map/all_gather | solution.py:13
  61.0 25.4 %copy-start.1 = (bf16[512,1536]{1,0:T(8,128)(2,1)S(1)}, bf16[512,1536]{1,0:T(8,128)(2,1)}, u32[]{:S(2)}) copy-start(bf16[512,1536]{1,0:T(8,128)(2,1)} %param.20) | copy-start | bytes 4718596
  92.0 5.3 %copy-start.5 = (f32[512]{0:T(512)S(1)}, f32[512]{0:T(512)}, u32[]{:S(2)}) copy-start(f32[512]{0:T(512)} %param.19) | copy-start | bytes 6148
  199.4 6.8 %copy-start.4 = (f32[1536]{0:T(1024)S(1)}, f32[1536]{0:T(1024)}, u32[]{:S(2)}) copy-start(f32[1536]{0:T(1024)} %param.21) | copy-start | bytes 18436
  206.1 4.0 %copy-start.2 = (bf16[129,1536]{1,0:T(8,128)(2,1)S(1)}, bf16[129,1536]{1,0:T(8,128)(2,1)}, u32[]{:S(2)}) copy-start(bf16[129,1536]{1,0:T(8,128)(2,1)} %scatter_custom_fusion) | copy-start | bytes 1188868
  207.5 4.3 %copy-start.3 = (f32[128,1536]{1,0:T(8,128)}, f32[128,1536]{1,0:T(8,128)S(1)}, u32[]{:S(2)}) copy-start(f32[128,1536]{1,0:T(8,128)S(1)} %convert_subtract_fusion) | copy-start | bytes 2359300
Sparse Core Ops, SparseCore 0:
  100.7 98.6 all-gather.3
